TPU v7x, 256 devices: a whole 4x4x8 slice. The times are simulated.
256 devices in a mesh: sector: 8 (over y, core), inner: 32 (over x, z).
Axes of the slice: x: 4, y: 4, z: 8, core: 2. Of those that a mesh axis runs over, the one named last changes fastest.
Arguments:
- density: float32 [128, 64, 16384], P('inner', None, 'sector'), may hold values from -6 to 6
- source_sector: int32 [32, 8, 16], P('inner'), may hold values from 0 to 7, as said below
- source_tile: int32 [32, 8, 16], P('inner'), may hold values from 0 to 15
- matrix_id: int32 [32, 8, 16], P('inner'), may hold values from 0 to 31
- cubic_weights: float32 [32, 128, 128], replicated, may hold values from -0.6 to 1.5, as said below
- bin_cells: int32 [8, 32], P('sector'), may hold values from 1 to 128, 2048 in all within a row
- wave_level: float32 [8, 32], P('sector'), may hold values from 0.15 to 1
- energy_rate: float32 [128, 64], replicated, may hold values from 0.01 to 0.12
- pitch_rate: float32 [128, 64], replicated, may hold values from 0.01 to 0.12
Outputs:
- advanced: float32 [128, 64, 16384], P('inner', None, 'sector')
Inputs may be any that keep to these rules, and one draw needn't show every extreme that they name: `source_sector`: for every energy block and destination sector, at most 3 of its 16 tiles depart from any one sector, exactly 3 depart from one sector, and that sector lies one to three sectors below the destination, cyclically. `cubic_weights`: every row of every matrix sums to one.
All inputs are finite; a program needn't handle non-finite values.
Results may differ from a plain program's by a relative error of at most 0.000096.
Values sent between devices are 32-bit elements; how exact they have to be, the bound alone decides.
A program may use at most 128 MiB of HBM per device.

v0:
```python
import jax
import jax.numpy as jnp
from jax import lax
from jax.sharding import PartitionSpec as P

PASSES = 12


def order_within(sources):
    tile_count = sources.shape[1]
    same = sources[:, :, None] == sources[:, None, :]
    earlier = jnp.arange(tile_count)[None, :] < jnp.arange(tile_count)[:, None]
    return jnp.sum((same & earlier[None]).astype(jnp.int32), axis=2)


def drift_step(density, source_sector, source_tile, matrix_id, cubic_weights):
    sectors = lax.axis_size("sector")
    sector_here = lax.axis_index("sector")
    energies, pitches, cell_count = density.shape
    tile_len = cubic_weights.shape[1]
    tile_count = cell_count // tile_len
    slot_count = max(2, (3 * tile_count + 2 * sectors - 1) // (2 * sectors))
    sources = source_sector[0]
    picked_tiles = source_tile[0]
    matrix_ids = matrix_id[0]
    tile_ranks = order_within(sources)
    slot_rank = jnp.arange(slot_count, dtype=jnp.int32)
    matched = (sources[:, None, :] == sector_here) & (
        tile_ranks[:, None, :] == slot_rank[None, :, None]
    )
    chosen = jnp.sum(jnp.where(matched, picked_tiles[:, None, :], 0), axis=2).reshape(-1)
    filled = jnp.any(matched, axis=2).reshape(-1).astype(jnp.float32)
    blocks = density.reshape(energies, pitches, tile_count, tile_len)
    outgoing = jnp.take(blocks, chosen, axis=2) * filled[None, None, :, None]
    incoming = lax.all_to_all(outgoing, "sector", split_axis=2, concat_axis=2, tiled=True)
    own_sources = sources[sector_here]
    own_ranks = tile_ranks[sector_here]
    own_ids = matrix_ids[sector_here]
    where_from = own_sources * slot_count + own_ranks
    departing = jnp.take(incoming, where_from, axis=2)
    matrices = jnp.take(cubic_weights, own_ids, axis=0)
    drifted = jnp.einsum("eptj,tij->epti", departing, matrices, precision=lax.Precision.HIGHEST)
    return drifted.reshape(energies, pitches, cell_count)


def one_pass(field, rate_cell, energy_rate, pitch_rate):
    flux_e = energy_rate[:-1, :, None] * (field[1:] - field[:-1])
    flux_p = pitch_rate[:, :-1, None] * (field[:, 1:] - field[:, :-1])
    change_e = jnp.pad(flux_e, ((0, 1), (0, 0), (0, 0))) - jnp.pad(flux_e, ((1, 0), (0, 0), (0, 0)))
    change_p = jnp.pad(flux_p, ((0, 0), (0, 1), (0, 0))) - jnp.pad(flux_p, ((0, 0), (1, 0), (0, 0)))
    return field + rate_cell[None, None, :] * (change_e + change_p)


def shards(
    density,
    source_sector,
    source_tile,
    matrix_id,
    cubic_weights,
    bin_cells,
    wave_level,
    energy_rate,
    pitch_rate,
):
    first = drift_step(density, source_sector, source_tile, matrix_id, cubic_weights)
    inner_count = lax.axis_size("inner")
    inner_here = lax.axis_index("inner")
    cell_count = first.shape[2]
    lengths = bin_cells[0]
    per_device = cell_count // inner_count
    owner_cells = jnp.full((inner_count,), per_device, jnp.int32)
    owner_ends = jnp.cumsum(owner_cells)
    owner_starts = owner_ends - owner_cells
    offsets = jnp.arange(per_device, dtype=jnp.int32)
    cell_index = owner_starts[:, None] + offsets[None, :]
    valid = (offsets[None, :] < owner_cells[:, None]).reshape(-1).astype(jnp.float32)
    clipped = jnp.minimum(cell_index, cell_count - 1).reshape(-1)
    packed = jnp.take(first, clipped, axis=2) * valid[None, None, :]
    cellwise = lax.all_to_all(packed, "inner", split_axis=2, concat_axis=0, tiled=True)
    bin_ends = jnp.cumsum(lengths)
    global_cells = owner_starts[inner_here] + offsets
    is_live = (offsets < owner_cells[inner_here]).astype(jnp.float32)
    bin_of = jnp.sum((bin_ends[None, :] <= global_cells[:, None]).astype(jnp.int32), axis=1)
    onehot = bin_of[:, None] == jnp.arange(inner_count, dtype=jnp.int32)[None, :]
    cell_level = jnp.sum(jnp.where(onehot, wave_level[0][None, :], 0.0), axis=1) * is_live

    def loop_body(step, current):
        return one_pass(current, cell_level, energy_rate, pitch_rate)

    diffused = lax.fori_loop(0, PASSES, loop_body, cellwise)
    returned = lax.all_to_all(diffused, "inner", split_axis=0, concat_axis=2, tiled=True)
    every_cell = jnp.arange(cell_count, dtype=jnp.int32)
    owner_index = jnp.sum((owner_ends[None, :] <= every_cell[:, None]).astype(jnp.int32), axis=1)
    offset = every_cell - owner_starts[owner_index]
    position = owner_index * per_device + offset
    restored = jnp.take(returned, position, axis=2)
    return drift_step(restored, source_sector, source_tile, matrix_id, cubic_weights)


def solution(mesh):
    return jax.shard_map(
        shards,
        mesh=mesh,
        in_specs=(
            P("inner", None, "sector"),
            P("inner", None, None),
            P("inner", None, None),
            P("inner", None, None),
            P(),
            P("sector", None),
            P("sector", None),
            P(),
            P(),
        ),
        out_specs=P("inner", None, "sector"),
        check_vma=False,
    )
```

profile of v0, /device:TPU:1, one launch (start us, length us, event | category | flops | bytes accessed | tf_op | source)
XLA Modules:
  0.0 494.0 jit_solution(5908928833812959469)
XLA Ops:
  4.9 4.0 gather_fusion.1
  8.9 4.3 bitcast_multiply_fusion.2
  13.2 7.6 %all-to-all-start = ((f32[4,64,24,128]{3,1,0,2:T(8,128)}), f32[4,64,24,128]{3,1,0,2:T(8,128)}, u32[]{:S(2)}, u32[]{:S(2)}) async-start(f32[4,64,24,128]{3,1,0,2:T(8,128)} %bitcast_multiply_fusion.2), calls=%async_computation | async-start | bytes 6291456 | tf_op jit(solution)/shard_map/all_to_all | solution.py:35
  23.2 35.2 %all-to-all-done = f32[4,64,24,128]{3,1,0,2:T(8,128)} async-done(((f32[4,64,24,128]{3,1,0,2:T(8,128)}), f32[4,64,24,128]{3,1,0,2:T(8,128)}, u32[]{:S(2)}, u32[]{:S(2)}) %all-to-all-start) | async-done | bytes 3145760 | tf_op jit(solution)/shard_map/all_to_all | solution.py:35
  58.5 4.0 copy.42
  67.3 3.2 copy.55
  70.5 17.5 %gather_fusion.3 = f32[2048,4,64]{2,1,0:T(4,128)} fusion(f32[4,64,2048]{1,0,2:T(4,128)} %bitcast.121, s32[2048]{0:T(1024)S(1)} %fusion.11), kind=kCustom, calls=%fused_computation.3.clone | custom fusion | bytes 4202496 | tf_op jit(solution)/shard_map/jit(_take)/gather | solution.py:78
  88.0 11.7 %fusion.21 = f32[2048,4,64]{2,1,0:T(4,128)} fusion(f32[2048]{0:T(1024)S(1)} %convert_element_type.47, f32[2048,4,64]{2,1,0:T(4,128)} %gather_fusion.3, pred[2048]{0:T(1024)(128)(4,1)S(1)} %compare_and_fusion.1), kind=kLoop, calls=%fused_computation.105 | loop fusion | flops 1048576 | bytes 4204544
  99.7 6.3 %reshape.380 = f32[32,1,16384]{2,1,0:T(1,128)} reshape(f32[2048,4,64]{2,1,0:T(4,128)} %fusion.21) | data formatting | bytes 4194304
  106.0 9.8 %all-to-all-start.1 = ((f32[32,1,16384]{2,1,0:T(1,128)}), f32[32,1,16384]{2,1,0:T(1,128)S(1)}, u32[]{:S(2)}, u32[]{:S(2)}) async-start(f32[32,1,16384]{2,1,0:T(1,128)} %reshape.380), calls=%async_computation.1 | async-start | bytes 4194304 | tf_op jit(solution)/shard_map/all_to_all | solution.py:79
  117.9 46.4 %all-to-all-done.1 = f32[32,1,16384]{2,1,0:T(1,128)S(1)} async-done(((f32[32,1,16384]{2,1,0:T(1,128)}), f32[32,1,16384]{2,1,0:T(1,128)S(1)}, u32[]{:S(2)}, u32[]{:S(2)}) %all-to-all-start.1) | async-done | bytes 2097184 | tf_op jit(solution)/shard_map/all_to_all | solution.py:79
  166.1 7.3 %reduce.51 = f32[32,16384]{1,0:T(8,128)S(1)} reduce(f32[32,1,16384]{2,1,0:T(1,128)} %copy-done.4, f32[]{:T(128)} %broadcast.519), dimensions={1}, to_apply=%all_to_all.33.reduce_sub_computation | reduce | bytes 4194308 | tf_op jit(solution)/shard_map/all_to_all | solution.py:79
  173.4 4.2 reshape.381
  177.7 5.2 %copy.57 = f32[4,64,32,64]{3,1,0,2:T(8,128)} copy(f32[4,64,32,64]{1,0,3,2:T(4,128)} %bitcast.119) | data formatting | bytes 4194304 | tf_op jit(solution)/shard_map/all_to_all | solution.py:79
  182.9 146.8 %while.12 = (s32[]{:T(128)}, f32[128,64,64]{2,1,0:T(8,128)}, f32[64]{0:T(128)S(1)}, f32[128,64]{1,0:T(8,128)S(1)}, f32[128,64]{1,0:T(8,128)S(1)}, /*index=5*/s32[]{:T(128)}) while((s32[]{:T(128)}, f32[128,64,64]{2,1,0:T(8,128)}, f32[64]{0:T(128)S(1)}, f32[128,64]{1,0:T(8,128)S(1)}, f32[128,64]{1,0:T(8,128)S(1)}, /*index=5*/s32[]{:T(128)}) %tuple.96), condition=%wide.region_7.12_spmd, body=%wide.region_6.11_spmd.sunk | while | flops 4694018 | bytes 37617276 | solution.py:90
  182.9 5.5 %subtract_multiply_fusion.4 = f32[128,63,64]{2,1,0:T(8,128)S(1)} fusion(f32[128,64,64]{2,1,0:T(8,128)} %get-tuple-element.209, f32[128,63]{1,0:T(8,128)S(1)} %bitcast.128), kind=kLoop, calls=%fused_computation.8.clone.1 | loop fusion | flops 1032192 | bytes 6225408 | tf_op jit(solution)/shard_map/while/body/eval_jaxpr/mul | solution.py:48
  190.2 3.0 multiply_add_fusion.2
  195.1 5.5 %subtract_multiply_fusion.4 = f32[128,63,64]{2,1,0:T(8,128)S(1)} fusion(f32[128,64,64]{2,1,0:T(8,128)} %get-tuple-element.209, f32[128,63]{1,0:T(8,128)S(1)} %bitcast.128), kind=kLoop, calls=%fused_computation.8.clone.1 | loop fusion | flops 1032192 | bytes 6225408 | tf_op jit(solution)/shard_map/while/body/eval_jaxpr/mul | solution.py:48
  202.5 3.0 multiply_add_fusion.2
  207.4 5.5 %subtract_multiply_fusion.4 = f32[128,63,64]{2,1,0:T(8,128)S(1)} fusion(f32[128,64,64]{2,1,0:T(8,128)} %get-tuple-element.209, f32[128,63]{1,0:T(8,128)S(1)} %bitcast.128), kind=kLoop, calls=%fused_computation.8.clone.1 | loop fusion | flops 1032192 | bytes 6225408 | tf_op jit(solution)/shard_map/while/body/eval_jaxpr/mul | solution.py:48
  214.7 3.0 multiply_add_fusion.2
  219.6 5.5 %subtract_multiply_fusion.4 = f32[128,63,64]{2,1,0:T(8,128)S(1)} fusion(f32[128,64,64]{2,1,0:T(8,128)} %get-tuple-element.209, f32[128,63]{1,0:T(8,128)S(1)} %bitcast.128), kind=kLoop, calls=%fused_computation.8.clone.1 | loop fusion | flops 1032192 | bytes 6225408 | tf_op jit(solution)/shard_map/while/body/eval_jaxpr/mul | solution.py:48
  226.9 3.0 multiply_add_fusion.2
  231.8 5.5 %subtract_multiply_fusion.4 = f32[128,63,64]{2,1,0:T(8,128)S(1)} fusion(f32[128,64,64]{2,1,0:T(8,128)} %get-tuple-element.209, f32[128,63]{1,0:T(8,128)S(1)} %bitcast.128), kind=kLoop, calls=%fused_computation.8.clone.1 | loop fusion | flops 1032192 | bytes 6225408 | tf_op jit(solution)/shard_map/while/body/eval_jaxpr/mul | solution.py:48
  239.2 3.0 multiply_add_fusion.2
  244.1 5.5 %subtract_multiply_fusion.4 = f32[128,63,64]{2,1,0:T(8,128)S(1)} fusion(f32[128,64,64]{2,1,0:T(8,128)} %get-tuple-element.209, f32[128,63]{1,0:T(8,128)S(1)} %bitcast.128), kind=kLoop, calls=%fused_computation.8.clone.1 | loop fusion | flops 1032192 | bytes 6225408 | tf_op jit(solution)/shard_map/while/body/eval_jaxpr/mul | solution.py:48
  251.4 3.0 multiply_add_fusion.2
  256.3 5.5 %subtract_multiply_fusion.4 = f32[128,63,64]{2,1,0:T(8,128)S(1)} fusion(f32[128,64,64]{2,1,0:T(8,128)} %get-tuple-element.209, f32[128,63]{1,0:T(8,128)S(1)} %bitcast.128), kind=kLoop, calls=%fused_computation.8.clone.1 | loop fusion | flops 1032192 | bytes 6225408 | tf_op jit(solution)/shard_map/while/body/eval_jaxpr/mul | solution.py:48
  263.6 3.0 multiply_add_fusion.2
  268.5 5.5 %subtract_multiply_fusion.4 = f32[128,63,64]{2,1,0:T(8,128)S(1)} fusion(f32[128,64,64]{2,1,0:T(8,128)} %get-tuple-element.209, f32[128,63]{1,0:T(8,128)S(1)} %bitcast.128), kind=kLoop, calls=%fused_computation.8.clone.1 | loop fusion | flops 1032192 | bytes 6225408 | tf_op jit(solution)/shard_map/while/body/eval_jaxpr/mul | solution.py:48
  275.9 3.0 multiply_add_fusion.2
  280.8 5.5 %subtract_multiply_fusion.4 = f32[128,63,64]{2,1,0:T(8,128)S(1)} fusion(f32[128,64,64]{2,1,0:T(8,128)} %get-tuple-element.209, f32[128,63]{1,0:T(8,128)S(1)} %bitcast.128), kind=kLoop, calls=%fused_computation.8.clone.1 | loop fusion | flops 1032192 | bytes 6225408 | tf_op jit(solution)/shard_map/while/body/eval_jaxpr/mul | solution.py:48
  288.1 3.0 multiply_add_fusion.2
  293.0 5.5 %subtract_multiply_fusion.4 = f32[128,63,64]{2,1,0:T(8,128)S(1)} fusion(f32[128,64,64]{2,1,0:T(8,128)} %get-tuple-element.209, f32[128,63]{1,0:T(8,128)S(1)} %bitcast.128), kind=kLoop, calls=%fused_computation.8.clone.1 | loop fusion | flops 1032192 | bytes 6225408 | tf_op jit(solution)/shard_map/while/body/eval_jaxpr/mul | solution.py:48
  305.3 5.5 %subtract_multiply_fusion.4 = f32[128,63,64]{2,1,0:T(8,128)S(1)} fusion(f32[128,64,64]{2,1,0:T(8,128)} %get-tuple-element.209, f32[128,63]{1,0:T(8,128)S(1)} %bitcast.128), kind=kLoop, calls=%fused_computation.8.clone.1 | loop fusion | flops 1032192 | bytes 6225408 | tf_op jit(solution)/shard_map/while/body/eval_jaxpr/mul | solution.py:48
  317.5 5.5 %subtract_multiply_fusion.4 = f32[128,63,64]{2,1,0:T(8,128)S(1)} fusion(f32[128,64,64]{2,1,0:T(8,128)} %get-tuple-element.209, f32[128,63]{1,0:T(8,128)S(1)} %bitcast.128), kind=kLoop, calls=%fused_computation.8.clone.1 | loop fusion | flops 1032192 | bytes 6225408 | tf_op jit(solution)/shard_map/while/body/eval_jaxpr/mul | solution.py:48
  329.7 5.5 %reshape.382 = f32[32,1,16384]{2,1,0:T(1,128)} reshape(f32[128,64,64]{2,1,0:T(8,128)} %get-tuple-element.74) | data formatting | bytes 4194304
  335.2 7.5 %all-to-all-start.2 = ((f32[32,1,16384]{2,1,0:T(1,128)}), f32[32,1,16384]{2,1,0:T(1,128)}, u32[]{:S(2)}, u32[]{:S(2)}) async-start(f32[32,1,16384]{2,1,0:T(1,128)} %reshape.382), calls=%async_computation.2 | async-start | bytes 4194304 | tf_op jit(solution)/shard_map/all_to_all | solution.py:91
  343.5 4.5 compare_select_fusion.1
  348.6 15.5 %compare_and_fusion = (pred[2048]{0:T(1024)(128)(4,1)S(1)}, s32[2048]{0:T(1024)S(1)}) fusion(pred[2048]{0:T(1024)(128)(4,1)S(1)} %get-tuple-element.119, pred[2048]{0:T(1024)(128)(4,1)S(1)} %get-tuple-element.118, pred[2048]{0:T(1024)(128)(4,1)S(1)} %get-tuple-element.117, pred[2048]{0:T(1024)(128)(4,1)S(1)} %get-tuple-element.116, ...), kind=kLoop, calls=%fused_computation.74 | loop fusion | flops 69632 | bytes 77924 | tf_op jit(solution)/shard_map/jit(_take)/and | solution.py:96
  364.1 27.0 %all-to-all-done.2 = f32[32,1,16384]{2,1,0:T(1,128)} async-done(((f32[32,1,16384]{2,1,0:T(1,128)}), f32[32,1,16384]{2,1,0:T(1,128)}, u32[]{:S(2)}, u32[]{:S(2)}) %all-to-all-start.2) | async-done | bytes 2097184 | tf_op jit(solution)/shard_map/all_to_all | solution.py:91
  391.1 7.3 %reduce.52 = f32[32,16384]{1,0:T(8,128)S(1)} reduce(f32[32,1,16384]{2,1,0:T(1,128)} %all-to-all-done.2, f32[]{:T(128)} %broadcast.519), dimensions={1}, to_apply=%all_to_all.37.reduce_sub_computation | reduce | bytes 4194308 | tf_op jit(solution)/shard_map/all_to_all | solution.py:91
  398.4 3.0 reshape.383
  401.5 5.2 %copy.58 = f32[4,64,32,64]{1,0,3,2:T(4,128)} copy(f32[4,64,32,64]{3,1,0,2:T(8,128)} %bitcast.120) | data formatting | bytes 4194304 | tf_op jit(solution)/shard_map/all_to_all | solution.py:91
  406.7 17.5 %gather_fusion.4 = f32[2048,4,64]{2,1,0:T(4,128)} fusion(f32[4,64,2048]{1,0,2:T(4,128)} %bitcast.122, s32[2048]{0:T(1024)S(1)} %broadcast_clamp_fusion), kind=kCustom, calls=%fused_computation.6.clone | custom fusion | bytes 4202496 | tf_op jit(solution)/shard_map/jit(_take)/gather | solution.py:96
  424.2 10.9 %broadcast_select_fusion = f32[2048,4,64]{2,1,0:T(4,128)} fusion(f32[2048,4,64]{2,1,0:T(4,128)} %gather_fusion.4, pred[2048]{0:T(1024)(128)(4,1)S(1)} %get-tuple-element.130), kind=kLoop, calls=%fused_computation.15 | loop fusion | flops 524288 | bytes 4196352 | tf_op jit(solution)/shard_map/jit(_take)/select_n | solution.py:96
  435.1 3.5 copy.52
  443.4 42.2 %all_to_all.46 = f32[4,64,24,128]{3,1,0,2:T(8,128)S(1)} all-to-all(f32[4,64,24,128]{3,1,0,2:T(8,128)S(1)} %bitcast_multiply_fusion.1), channel_id=1, replica_groups=mesh['sector'=8,'inner'=32] {'sector'}, dimensions={2} | all-to-all | bytes 6291456 | tf_op jit(solution)/shard_map/all_to_all | solution.py:35
  (132 shorter events, 84.1 us)
Async XLA Ops:
  0.0 3.1 copy-start
  13.2 8.6 %copy-start.5 = (f32[32,128,128]{2,1,0:T(8,128)S(1)}, f32[32,128,128]{2,1,0:T(8,128)}, u32[]{:S(2)}) copy-start(f32[32,128,128]{2,1,0:T(8,128)} %param.23) | copy-start | bytes 6291460
  13.2 45.2 %all-to-all-start = ((f32[4,64,24,128]{3,1,0,2:T(8,128)}), f32[4,64,24,128]{3,1,0,2:T(8,128)}, u32[]{:S(2)}, u32[]{:S(2)}) async-start(f32[4,64,24,128]{3,1,0,2:T(8,128)} %bitcast_multiply_fusion.2), calls=%async_computation | async-start | bytes 6291456 | tf_op jit(solution)/shard_map/all_to_all | solution.py:35
  106.0 9.8 %copy-start.8 = (s32[1,32]{1,0:T(1,128)S(1)}, s32[1,32]{1,0:T(1,128)}, u32[]{:S(2)}) copy-start(s32[1,32]{1,0:T(1,128)} %param.24) | copy-start | bytes 388
  106.0 10.1 %copy-start.6 = (f32[128,64]{0,1:T(8,128)S(1)}, f32[128,64]{0,1:T(8,128)}, u32[]{:S(2)}) copy-start(f32[128,64]{0,1:T(8,128)} %param.26) | copy-start | bytes 98308
  106.0 10.2 %copy-start.7 = (f32[128,64]{0,1:T(8,128)S(1)}, f32[128,64]{0,1:T(8,128)}, u32[]{:S(2)}) copy-start(f32[128,64]{0,1:T(8,128)} %param.27) | copy-start | bytes 98308
  106.0 11.8 %copy-start.9 = (f32[1,32]{1,0:T(1,128)S(1)}, f32[1,32]{1,0:T(1,128)}, u32[]{:S(2)}) copy-start(f32[1,32]{1,0:T(1,128)} %param.25) | copy-start | bytes 388
  106.0 58.3 %all-to-all-start.1 = ((f32[32,1,16384]{2,1,0:T(1,128)}), f32[32,1,16384]{2,1,0:T(1,128)S(1)}, u32[]{:S(2)}, u32[]{:S(2)}) async-start(f32[32,1,16384]{2,1,0:T(1,128)} %reshape.380), calls=%async_computation.1 | async-start | bytes 4194304 | tf_op jit(solution)/shard_map/all_to_all | solution.py:79
  164.3 1.3 copy-start.4
  182.9 5.5 %copy-start.2 = (f32[128,64,64]{2,1,0:T(8,128)S(1)}, f32[128,64,64]{2,1,0:T(8,128)}, u32[]{:S(2)}) copy-start(f32[128,64,64]{2,1,0:T(8,128)} %get-tuple-element.209) | copy-start | bytes 6291460 | tf_op jit(solution)/shard_map/while
  193.2 1.9 copy-start.3
  195.1 5.5 %copy-start.2 = (f32[128,64,64]{2,1,0:T(8,128)S(1)}, f32[128,64,64]{2,1,0:T(8,128)}, u32[]{:S(2)}) copy-start(f32[128,64,64]{2,1,0:T(8,128)} %get-tuple-element.209) | copy-start | bytes 6291460 | tf_op jit(solution)/shard_map/while
  205.4 1.9 copy-start.3
  207.4 5.5 %copy-start.2 = (f32[128,64,64]{2,1,0:T(8,128)S(1)}, f32[128,64,64]{2,1,0:T(8,128)}, u32[]{:S(2)}) copy-start(f32[128,64,64]{2,1,0:T(8,128)} %get-tuple-element.209) | copy-start | bytes 6291460 | tf_op jit(solution)/shard_map/while
  217.7 1.9 copy-start.3
  219.6 5.5 %copy-start.2 = (f32[128,64,64]{2,1,0:T(8,128)S(1)}, f32[128,64,64]{2,1,0:T(8,128)}, u32[]{:S(2)}) copy-start(f32[128,64,64]{2,1,0:T(8,128)} %get-tuple-element.209) | copy-start | bytes 6291460 | tf_op jit(solution)/shard_map/while
  229.9 1.9 copy-start.3
  231.8 5.5 %copy-start.2 = (f32[128,64,64]{2,1,0:T(8,128)S(1)}, f32[128,64,64]{2,1,0:T(8,128)}, u32[]{:S(2)}) copy-start(f32[128,64,64]{2,1,0:T(8,128)} %get-tuple-element.209) | copy-start | bytes 6291460 | tf_op jit(solution)/shard_map/while
  242.1 1.9 copy-start.3
  244.1 5.5 %copy-start.2 = (f32[128,64,64]{2,1,0:T(8,128)S(1)}, f32[128,64,64]{2,1,0:T(8,128)}, u32[]{:S(2)}) copy-start(f32[128,64,64]{2,1,0:T(8,128)} %get-tuple-element.209) | copy-start | bytes 6291460 | tf_op jit(solution)/shard_map/while
  254.4 1.9 copy-start.3
  256.3 5.5 %copy-start.2 = (f32[128,64,64]{2,1,0:T(8,128)S(1)}, f32[128,64,64]{2,1,0:T(8,128)}, u32[]{:S(2)}) copy-start(f32[128,64,64]{2,1,0:T(8,128)} %get-tuple-element.209) | copy-start | bytes 6291460 | tf_op jit(solution)/shard_map/while
  266.6 1.9 copy-start.3
  268.5 5.5 %copy-start.2 = (f32[128,64,64]{2,1,0:T(8,128)S(1)}, f32[128,64,64]{2,1,0:T(8,128)}, u32[]{:S(2)}) copy-start(f32[128,64,64]{2,1,0:T(8,128)} %get-tuple-element.209) | copy-start | bytes 6291460 | tf_op jit(solution)/shard_map/while
  278.9 1.9 copy-start.3
  280.8 5.5 %copy-start.2 = (f32[128,64,64]{2,1,0:T(8,128)S(1)}, f32[128,64,64]{2,1,0:T(8,128)}, u32[]{:S(2)}) copy-start(f32[128,64,64]{2,1,0:T(8,128)} %get-tuple-element.209) | copy-start | bytes 6291460 | tf_op jit(solution)/shard_map/while
  291.1 1.9 copy-start.3
  293.0 5.5 %copy-start.2 = (f32[128,64,64]{2,1,0:T(8,128)S(1)}, f32[128,64,64]{2,1,0:T(8,128)}, u32[]{:S(2)}) copy-start(f32[128,64,64]{2,1,0:T(8,128)} %get-tuple-element.209) | copy-start | bytes 6291460 | tf_op jit(solution)/shard_map/while
  303.3 1.9 copy-start.3
  305.3 5.5 %copy-start.2 = (f32[128,64,64]{2,1,0:T(8,128)S(1)}, f32[128,64,64]{2,1,0:T(8,128)}, u32[]{:S(2)}) copy-start(f32[128,64,64]{2,1,0:T(8,128)} %get-tuple-element.209) | copy-start | bytes 6291460 | tf_op jit(solution)/shard_map/while
  315.6 1.9 copy-start.3
  317.5 5.5 %copy-start.2 = (f32[128,64,64]{2,1,0:T(8,128)S(1)}, f32[128,64,64]{2,1,0:T(8,128)}, u32[]{:S(2)}) copy-start(f32[128,64,64]{2,1,0:T(8,128)} %get-tuple-element.209) | copy-start | bytes 6291460 | tf_op jit(solution)/shard_map/while
  327.8 1.9 copy-start.3
  335.2 55.9 %all-to-all-start.2 = ((f32[32,1,16384]{2,1,0:T(1,128)}), f32[32,1,16384]{2,1,0:T(1,128)}, u32[]{:S(2)}, u32[]{:S(2)}) async-start(f32[32,1,16384]{2,1,0:T(1,128)} %reshape.382), calls=%async_computation.2 | async-start | bytes 4194304 | tf_op jit(solution)/shard_map/all_to_all | solution.py:91
  490.3 3.7 copy-start.1
where the time goes:
time: 496 us; the launch traced here: 494 us
  other arithmetic  194 us (39%)
  local copies, waits for them, and re-layouts  120 us (24%)
  waiting for transfers between devices  109 us (22%)
  blocking collectives  42.2 us (9%)
  starting transfers between devices  24.9 us (5%)
    mul x12, other arithmetic, one_pass(): flux_p = pitch_rate[:, :-1, None] * (field[:, 1:] - field[:, :-1])  65.8 us
    all_to_all x1, waiting for transfers between devices, shards(): lax.all_to_all(packed, 'inner', split_axis=2, concat_axis=0, tiled=True)  46.4 us
    all_to_all x1, blocking collectives, drift_step(): lax.all_to_all(outgoing, 'sector', split_axis=2, concat_axis=2, tiled=True)  42.2 us
    add x12, other arithmetic, one_pass(): return field + rate_cell[None, None, :] * (change_e + change_p)  35.7 us
    all_to_all x1, waiting for transfers between devices, drift_step(): lax.all_to_all(outgoing, 'sector', split_axis=2, concat_axis=2, tiled=True)  35.2 us
    all_to_all x1, waiting for transfers between devices, shards(): lax.all_to_all(diffused, 'inner', split_axis=0, concat_axis=2, tiled=True)  27 us
    while x48, local copies, waits for them, and re-layouts  23.1 us
    mul x12, other arithmetic, one_pass(): flux_e = energy_rate[:-1, :, None] * (field[1:] - field[:-1])  21.8 us
  transfers between devices with their start and end apart: 3, of which 3 were waited for; matrix products, arithmetic and copies ran while one was open for 5% of the time, Pallas kernels for 0%

commit v1 on v0

v1 whole, which is shorter than its diff:
```python
import functools

import jax
import jax.numpy as jnp
from jax import lax
from jax.experimental import pallas as pl
from jax.experimental.pallas import tpu as pltpu
from jax.sharding import PartitionSpec as P

PASSES = 12
MESH = pl.DeviceIdType.MESH
F32 = jnp.float32
BF16 = jnp.bfloat16


def split(value):
    high = value.astype(BF16)
    low = (value - high.astype(F32)).astype(BF16)
    return high, low


def swap_halves(upper, lower, first_half):
    upper_rolled = pltpu.roll(upper, 64, 2)
    lower_rolled = pltpu.roll(lower, 64, 2)
    return (
        jnp.where(first_half, upper, lower_rolled),
        jnp.where(first_half, upper_rolled, lower),
    )


def kernel(
    src_ref,
    tile_ref,
    mid_ref,
    bins_ref,
    wave_ref,
    dens_ref,
    weight_ref,
    er_ref,
    pr_ref,
    out_ref,
    pick_ref,
    slot_ref,
    natural,
    tiles,
    send1,
    recv1_0,
    recv1_1,
    recv1_2,
    recv1_3,
    gath,
    field,
    other,
    back_0,
    back_1,
    back_2,
    back_3,
    send2,
    recv2_0,
    recv2_1,
    recv2_2,
    recv2_3,
    coef_e,
    coef_p,
    wprep,
    s_a,
    r_a,
    s_c,
    r_c,
    s_e,
    r_e,
    s_f,
    r_f,
):
    recv1 = (recv1_0, recv1_1, recv1_2, recv1_3)
    back = (back_0, back_1, back_2, back_3)
    recv2 = (recv2_0, recv2_1, recv2_2, recv2_3)
    s = lax.axis_index("sector")
    i = lax.axis_index("inner")

    def sector_at(m):
        return lax.rem(s + 3 * (m + 1), 8)

    barrier = pltpu.get_barrier_semaphore()
    for m in range(7):
        pl.semaphore_signal(barrier, inc=1, device_id=(sector_at(m), i), device_id_type=MESH)
    for off in range(1, 32):
        pl.semaphore_signal(
            barrier, inc=1, device_id=(s, lax.rem(i + off, 32)), device_id_type=MESH
        )

    for d in range(8):
        count = jnp.int32(0)
        picks = [jnp.int32(0)] * 3
        for t in range(16):
            hit = src_ref[d, t] == s
            tile = tile_ref[d, t]
            for r in range(3):
                picks[r] = jnp.where(hit & (count == r), tile, picks[r])
            count = count + hit.astype(jnp.int32)
        for r in range(3):
            pick_ref[d * 3 + r] = picks[r]

    for e in range(4):
        for t in range(16):
            natural[t] = dens_ref[e, :, t * 128 : (t + 1) * 128]
        for t in range(16):
            for half in range(2):
                for q in range(4):
                    to = half * 32 + q * 8
                    tiles[e, t, to : to + 8, :] = natural[
                        t, pl.ds(half * 32 + q, 8, stride=4), :
                    ]
        for m in range(7):
            for r in range(3):
                send1[e, m, r] = tiles[e, pick_ref[sector_at(m) * 3 + r]]
        for r in range(3):
            recv1[e][s * 3 + r] = tiles[e, pick_ref[s * 3 + r]]

    pl.semaphore_wait(barrier, 38)

    for e in range(4):

        def send_first(m, _, e=e):
            pltpu.make_async_remote_copy(
                send1.at[e, m],
                recv1[e].at[pl.ds(s * 3, 3)],
                s_a.at[e],
                r_a.at[e],
                device_id=(sector_at(m), i),
                device_id_type=MESH,
            ).start()
            return 0

        lax.fori_loop(0, 7, send_first, 0)

    own = [src_ref[s, t] for t in range(16)]
    for t in range(16):
        rank = jnp.int32(0)
        for u in range(t):
            rank = rank + (own[u] == own[t]).astype(jnp.int32)
        slot_ref[t] = own[t] * 3 + rank

    for t in range(16):
        high, low = split(weight_ref[mid_ref[s, t]].T)
        wprep[t, 0:128, 0:128] = high
        wprep[t, 128:256, 0:128] = high
        wprep[t, 0:128, 128:256] = low
        wprep[t, 128:256, 128:256] = low

    lanes = lax.broadcasted_iota(jnp.int32, (4, 8, 128), 2)
    first_half = lanes < 64

    def interpolate(rows, t):
        high, low = split(rows)
        both = jnp.dot(
            jnp.concatenate([high, low], axis=1), wprep[t], preferred_element_type=F32
        )
        return both[:, 0:128] + both[:, 128:256]

    def first_drift(e):
        pltpu.make_async_copy(
            recv1[e].at[pl.ds(0, 21)], recv1[e].at[pl.ds(0, 21)], r_a.at[e]
        ).wait()

        def halves(t):
            moved = interpolate(recv1[e][slot_ref[t]], t)
            return swap_halves(
                moved[0:32].reshape(4, 8, 128), moved[32:64].reshape(4, 8, 128), first_half
            )

        def send(place, target):
            pltpu.make_async_remote_copy(
                gath.at[e, place],
                field.at[i * 4 + e],
                s_c.at[e],
                r_c,
                device_id=(s, target),
                device_id_type=MESH,
            ).start()

        for step in range(15):
            t = lax.rem(i // 2 + 3 * (step + 1), 16)
            outs = halves(t)
            for half in range(2):
                gath[e, step * 2 + half] = outs[half]
                send(step * 2 + half, t * 2 + half)
        outs = halves(i // 2)
        odd = lax.rem(i, 2) == 1
        field[i * 4 + e] = jnp.where(odd, outs[1], outs[0])
        gath[e, 30] = jnp.where(odd, outs[0], outs[1])
        send(30, i + 1 - 2 * lax.rem(i, 2))

    for e in range(4):
        first_drift(e)

    lane_row = lax.broadcasted_iota(jnp.int32, (1, 128), 1)
    cell = i * 64 + lax.rem(lane_row, 64)
    level = jnp.zeros((1, 128), F32)
    start = jnp.int32(0)
    for k in range(32):
        level = jnp.where(cell >= start, wave_ref[0, k], level)
        start = start + bins_ref[0, k]
    row = lax.broadcasted_iota(jnp.int32, (32, 64), 0)
    pitch = lax.broadcasted_iota(jnp.int32, (32, 64), 1)
    chosen = lax.rem(pitch, 32) == lax.rem(row, 8) * 4 + row // 8
    mask_e = chosen.astype(F32)
    mask_p = (chosen & (pitch < 63)).astype(F32)
    half_of = (
        lax.broadcasted_iota(jnp.int32, (64, 128), 0) // 32
        == lax.broadcasted_iota(jnp.int32, (64, 128), 1) // 64
    ).astype(F32)
    sub = lax.broadcasted_iota(jnp.int32, (8, 64), 0)

    def spread(rates, mask):
        wide = (rates[:, None, :] * mask[None]).reshape(256, 64)
        full = jnp.dot(
            wide, half_of, precision=lax.Precision.HIGHEST, preferred_element_type=F32
        )
        return (full * level).reshape(8, 4, 8, 128)

    def coefficients(b, _):
        at = pl.ds(pl.multiple_of(b * 8, 8), 8)
        rates = jnp.where(b * 8 + sub < 127, er_ref[at, :], 0.0)
        coef_e[at] = spread(rates, mask_e)
        coef_p[at] = spread(pr_ref[at, :], mask_p)
        return 0

    lax.fori_loop(0, 16, coefficients, 0)
    field[128] = jnp.zeros((4, 8, 128), F32)
    other[128] = jnp.zeros((4, 8, 128), F32)

    pltpu.make_async_copy(field.at[pl.ds(0, 124)], field.at[pl.ds(0, 124)], r_c).wait()

    sublane = lax.broadcasted_iota(jnp.int32, (8, 128), 0)
    top, bottom = sublane == 0, sublane == 7

    def one_pass(source, target):
        def rows(b, carry):
            now, flux_before = carry
            for k in range(8):
                e = b * 8 + k
                later = source[e + 1]
                flux = coef_e[e] * (later - now)
                shifted = pltpu.roll(now[0], 7, 0)
                shifted = jnp.where(bottom, pltpu.roll(shifted, 64, 1), shifted)
                pitch_flux = [
                    coef_p[e, q] * ((now[q + 1] if q < 3 else shifted) - now[q])
                    for q in range(4)
                ]
                wrapped = pltpu.roll(pitch_flux[3], 1, 0)
                wrapped = jnp.where(top, pltpu.roll(wrapped, 64, 1), wrapped)
                for q in range(4):
                    below = pitch_flux[q - 1] if q else wrapped
                    target[e, q] = now[q] + (
                        (flux[q] - flux_before[q]) + (pitch_flux[q] - below)
                    )
                now, flux_before = later, flux
            return now, flux_before

        lax.fori_loop(0, 16, rows, (source[0], jnp.zeros((4, 8, 128), F32)))

    def two_passes(_, carry):
        one_pass(field, other)
        one_pass(other, field)
        return carry

    lax.fori_loop(0, PASSES // 2, two_passes, 0)

    for e in range(4):

        def send_back(n, _, e=e):
            target = lax.rem(i + 13 * (n + 1), 32)
            pltpu.make_async_remote_copy(
                field.at[target * 4 + e],
                back[e].at[i],
                s_e.at[e],
                r_e.at[e],
                device_id=(s, target),
                device_id_type=MESH,
            ).start()
            return 0

        lax.fori_loop(0, 31, send_back, 0)
        back[e][i] = field[i * 4 + e]

    def pack_second(e):
        pltpu.make_async_copy(
            back[e].at[pl.ds(0, 31)], back[e].at[pl.ds(0, 31)], r_e.at[e]
        ).wait()

        def pack(d, ref, lead, place):
            for r in range(3):
                tile = pick_ref[d * 3 + r]
                outs = swap_halves(back[e][tile * 2], back[e][tile * 2 + 1], first_half)
                for half in range(2):
                    for q in range(4):
                        at = pl.ds(half * 32 + q, 8, stride=4)
                        ref[(*lead, place + r, at, slice(None))] = outs[half][q]

        for m in range(7):
            d = sector_at(m)
            pack(d, send2, (e, m), 0)
            pltpu.make_async_remote_copy(
                send2.at[e, m],
                recv2[e].at[pl.ds(s * 3, 3)],
                s_f.at[e],
                r_f.at[e],
                device_id=(d, i),
                device_id_type=MESH,
            ).start()
        pack(s, recv2[e], (), s * 3)

    def second_drift(e):
        pltpu.make_async_copy(
            recv2[e].at[pl.ds(0, 21)], recv2[e].at[pl.ds(0, 21)], r_f.at[e]
        ).wait()

        for t in range(16):
            out_ref[e, :, t * 128 : (t + 1) * 128] = interpolate(recv2[e][slot_ref[t]], t)

    pack_second(0)
    for e in range(1, 4):
        pack_second(e)
        second_drift(e - 1)
    second_drift(3)

    def drain(e, _):
        pltpu.make_async_copy(send1.at[e, pl.ds(0, 7)], send1.at[e, pl.ds(0, 7)], s_a.at[e]).wait()
        pltpu.make_async_copy(gath.at[e, pl.ds(0, 31)], gath.at[e, pl.ds(0, 31)], s_c.at[e]).wait()
        pltpu.make_async_copy(field.at[pl.ds(0, 31)], field.at[pl.ds(0, 31)], s_e.at[e]).wait()
        pltpu.make_async_copy(send2.at[e, pl.ds(0, 7)], send2.at[e, pl.ds(0, 7)], s_f.at[e]).wait()
        return 0

    lax.fori_loop(0, 4, drain, 0)


def shards(
    density,
    source_sector,
    source_tile,
    matrix_id,
    cubic_weights,
    bin_cells,
    wave_level,
    energy_rate,
    pitch_rate,
):
    vmem = pl.BlockSpec(memory_space=pltpu.VMEM)
    smem = pl.BlockSpec(memory_space=pltpu.SMEM)
    dma = pltpu.SemaphoreType.DMA
    return pl.pallas_call(
        kernel,
        out_shape=jax.ShapeDtypeStruct((4, 64, 2048), F32),
        in_specs=[smem] * 5 + [vmem] * 4,
        out_specs=vmem,
        scratch_shapes=[
            pltpu.SMEM((24,), jnp.int32),
            pltpu.SMEM((16,), jnp.int32),
            pltpu.VMEM((16, 64, 128), F32),
            pltpu.VMEM((4, 16, 64, 128), F32),
            pltpu.VMEM((4, 7, 3, 64, 128), F32),
            *[pltpu.VMEM((24, 64, 128), F32)] * 4,
            pltpu.VMEM((4, 31, 4, 8, 128), F32),
            pltpu.VMEM((129, 4, 8, 128), F32),
            pltpu.VMEM((129, 4, 8, 128), F32),
            *[pltpu.VMEM((32, 4, 8, 128), F32)] * 4,
            pltpu.VMEM((4, 7, 3, 64, 128), F32),
            *[pltpu.VMEM((24, 64, 128), F32)] * 4,
            pltpu.VMEM((128, 4, 8, 128), F32),
            pltpu.VMEM((128, 4, 8, 128), F32),
            pltpu.VMEM((16, 256, 256), BF16),
            dma((4,)),
            dma((4,)),
            dma((4,)),
            dma,
            dma((4,)),
            dma((4,)),
            dma((4,)),
            dma((4,)),
        ],
        compiler_params=pltpu.CompilerParams(
            collective_id=0, has_side_effects=True, vmem_limit_bytes=50 * 2**20
        ),
        name="ion_step",
    )(
        source_sector[0],
        source_tile[0],
        matrix_id[0],
        bin_cells,
        wave_level,
        density,
        cubic_weights,
        energy_rate,
        pitch_rate,
    )


def solution(mesh):
    return jax.shard_map(
        shards,
        mesh=mesh,
        in_specs=(
            P("inner", None, "sector"),
            P("inner", None, None),
            P("inner", None, None),
            P("inner", None, None),
            P(),
            P("sector", None),
            P("sector", None),
            P(),
            P(),
        ),
        out_specs=P("inner", None, "sector"),
        check_vma=False,
    )
```

time: 496 us -> 167 us (0.34)
  other arithmetic: 194 us -> 0 us
  Pallas kernels: 0 us -> 159 us
  local copies, waits for them, and re-layouts: 120 us -> 6.39 us
  waiting for transfers between devices: 109 us -> 0 us
  blocking collectives: 42.2 us -> 0 us
  starting transfers between devices: 24.9 us -> 0 us
    pallas_call x0 -> x1, Pallas kernels: none -> 159 us  [shards(): pl.pallas_call(kernel, out_shape=jax.ShapeDtypeStruct((4, 64, 2048), F32)...]
    all_to_all x3 -> x0, waiting for transfers between devices: 109 us -> none  [the longest x1 46.4 us: shards(): lax.all_to_all(packed, 'inner', split_axis=2, concat_axis=0, tiled=True)]
    mul x27 -> x0, other arithmetic: 94.3 us -> none  [the longest x12 65.8 us: one_pass(): flux_p = pitch_rate[:, :-1, None] * (field[:, 1:] - field[:, :-1])]
    gather x9 -> x0, local copies, waits for them, and re-layouts: 48.7 us -> none  [the longest x1 17.5 us: shards(): packed = jnp.take(first, clipped, axis=2) * valid[None, None, :]]
    all_to_all x1 -> x0, blocking collectives: 42.2 us -> none  [drift_step(): lax.all_to_all(outgoing, 'sector', split_axis=2, concat_axis=2, tiled=True)]
    add x13 -> x0, other arithmetic: 36.4 us -> none  [the longest x12 35.7 us: one_pass(): return field + rate_cell[None, None, :] * (change_e + change_p)]
    all_to_all x3 -> x0, starting transfers between devices: 24.9 us -> none  [the longest x1 9.78 us: shards(): lax.all_to_all(packed, 'inner', split_axis=2, concat_axis=0, tiled=True)]
    while x50 -> x0, local copies, waits for them, and re-layouts: 23.2 us -> none
  transfers between devices with their start and end apart: 3 -> 0, of which waited for: 3 -> 0; matrix products, arithmetic and copies ran while one was open for 5% -> 0% of each run, Pallas kernels for 0% -> 0%
where the time goes in v1:
time: 167 us; the launch traced here: 166 us
  Pallas kernels  159 us (95%)
  local copies, waits for them, and re-layouts  6.39 us (4%)
    pallas_call x1, Pallas kernels, shards(): pl.pallas_call(kernel, out_shape=jax.ShapeDtypeStruct((4, 64, 2048), F32)...  159 us
    unnamed x13, local copies, waits for them, and re-layouts  6.39 us

profile of v1, /device:TPU:1, one launch (start us, length us, event | category | flops | bytes accessed | tf_op | source)
XLA Modules:
  0.0 165.9 jit_solution(6035942579614575234)
XLA Ops:
  0.0 0.8 copy.10.er_ref
  0.9 0.9 copy.11.pr_ref
  1.7 0.0 copy-start
  1.7 0.7 copy-done
  2.4 0.0 copy-start.1
  2.4 0.7 copy-done.1
  3.1 0.0 copy-start.2
  3.1 0.7 copy-done.2
  3.8 0.0 copy-start.3
  3.8 0.7 copy-done.3
  4.4 0.0 copy-start.4
  4.4 0.7 copy-done.4
  5.1 159.5 %ion_step.1 = f32[4,64,2048]{2,1,0:T(8,128)S(1)} custom-call(s32[8,16]{1,0:T(8,128)S(1)} %bitcast.3, s32[8,16]{1,0:T(8,128)S(1)} %bitcast.4, s32[8,16]{1,0:T(8,128)S(1)} %bitcast.5, s32[1,32]{1,0:T(1,128)S(1)} %copy-done.3, f32[1,32]{1,0:T(1,128)S(1)} %copy-done.4, f32[4,64,2048]{2,1,0:T(8,128)} %dens_ref.1, f32[32,128,128]{2,1,0:T(8,128)} %weight_ref.1, ...), custom_call_target="tpu_custom_call" | custom-call | tf_op jit(solution)/shard_map/ion_step/pallas_call | solution.py:352
  164.6 1.3 copy.13
Async XLA Ops:
  1.7 0.7 copy-start
  2.4 0.7 copy-start.1
  3.1 0.7 copy-start.2
  3.8 0.7 copy-start.3
  4.4 0.7 copy-start.4

commit v2 on v0

v2 whole, which is shorter than its diff:
```python
import jax
import jax.numpy as jnp
from jax import lax
from jax.experimental import pallas as pl
from jax.experimental.pallas import tpu as pltpu
from jax.sharding import PartitionSpec as P

PASSES = 12
MESH = pl.DeviceIdType.MESH
F32 = jnp.float32
BF16 = jnp.bfloat16


def split(value):
    high = value.astype(BF16)
    low = (value - high.astype(F32)).astype(BF16)
    return high, low


def turn(blocks, far, near):
    b0, b1, b2, b3 = blocks

    def exchange(low, high, first, width):
        return (
            jnp.where(first, low, pltpu.roll(high, width, 2)),
            jnp.where(first, pltpu.roll(low, 128 - width, 2), high),
        )

    b0, b2 = exchange(b0, b2, far, 64)
    b1, b3 = exchange(b1, b3, far, 64)
    b0, b1 = exchange(b0, b1, near, 32)
    b2, b3 = exchange(b2, b3, near, 32)
    return b0, b1, b2, b3


def kernel(*refs):
    refs = list(refs)

    def take(count):
        out = refs[:count]
        del refs[:count]
        return out

    (src_in, tile_in, mid_in, bins_in, wave_in, dens_in, weight_in, er_in, pr_in) = take(9)
    (out_ref,) = take(1)
    src_ref, tile_ref, mid_ref, bins_ref, wave_ref, pick_ref, slot_ref = take(7)
    natural = take(4)
    tiles, weight_ref, er_ref, pr_ref, er_rows, pr_rows, send1 = take(7)
    recv1 = take(4)
    (gath,) = take(1)
    field = take(2)
    (other,) = take(1)
    coef_e = take(2)
    coef_p = take(2)
    back = [take(4) for _ in range(2)]
    (send2,) = take(1)
    recv2 = [take(4) for _ in range(2)]
    wprep, order_buf = take(2)
    t_sem, d_sem, w_sem, s_a, r_a, s_c, r_c, s_e, r_e, s_f, r_f = take(11)

    s = lax.axis_index("sector")
    i = lax.axis_index("inner")

    def sector_at(m):
        return lax.rem(s + 3 * (m + 1), 8)

    barrier = pltpu.get_barrier_semaphore()
    for m in range(7):
        pl.semaphore_signal(barrier, inc=1, device_id=(sector_at(m), i), device_id_type=MESH)
    for off in range(1, 32):
        pl.semaphore_signal(
            barrier, inc=1, device_id=(s, lax.rem(i + off, 32)), device_id_type=MESH
        )

    tables = [
        pltpu.make_async_copy(a, b, t_sem.at[n])
        for n, (a, b) in enumerate(
            (
                (src_in, src_ref),
                (tile_in, tile_ref),
                (mid_in, mid_ref),
                (bins_in, bins_ref),
                (wave_in, wave_ref),
            )
        )
    ]
    for copy in tables:
        copy.start()
    for e in range(4):
        for t in range(16):
            pltpu.make_async_copy(
                dens_in.at[e, :, t * 128 : (t + 1) * 128], natural[e].at[t], d_sem.at[e]
            ).start()
    parameters = [
        pltpu.make_async_copy(a, b, w_sem.at[n])
        for n, (a, b) in enumerate(
            ((weight_in, weight_ref), (er_in, er_ref), (pr_in, pr_ref))
        )
    ]
    for copy in parameters:
        copy.start()
    for copy in tables:
        copy.wait()

    for d in range(8):
        count = jnp.int32(0)
        picks = [jnp.int32(0)] * 3
        for t in range(16):
            hit = src_ref[0, d, t] == s
            tile = tile_ref[0, d, t]
            for r in range(3):
                picks[r] = jnp.where(hit & (count == r), tile, picks[r])
            count = count + hit.astype(jnp.int32)
        for r in range(3):
            pick_ref[d * 3 + r] = picks[r]

    def pack_first(e):
        pltpu.make_async_copy(natural[e], natural[e], d_sem.at[e]).wait()
        for t in range(16):
            for quarter in range(4):
                for q in range(2):
                    to = quarter * 16 + q * 8
                    tiles[e, t, to : to + 8, :] = natural[e][
                        t, pl.ds(quarter * 16 + q, 8, stride=2), :
                    ]
        for m in range(7):
            for r in range(3):
                send1[e, m, r] = tiles[e, pick_ref[sector_at(m) * 3 + r]]
        for r in range(3):
            recv1[e][s * 3 + r] = tiles[e, pick_ref[s * 3 + r]]

    def send_first(e):
        def one(m, _):
            pltpu.make_async_remote_copy(
                send1.at[e, m],
                recv1[e].at[pl.ds(s * 3, 3)],
                s_a.at[e],
                r_a.at[e],
                device_id=(sector_at(m), i),
                device_id_type=MESH,
            ).start()
            return 0

        lax.fori_loop(0, 7, one, 0)

    pack_first(0)
    pl.semaphore_wait(barrier, 38)
    send_first(0)
    for e in range(1, 4):
        pack_first(e)
        send_first(e)

    own = [src_ref[0, s, t] for t in range(16)]
    for t in range(16):
        rank = jnp.int32(0)
        for u in range(t):
            rank = rank + (own[u] == own[t]).astype(jnp.int32)
        slot_ref[t] = own[t] * 3 + rank

    for copy in parameters:
        copy.wait()
    for t in range(16):
        high, low = split(weight_ref[mid_ref[0, s, t]].T)
        wprep[t, 0:128, 0:128] = high
        wprep[t, 128:256, 0:128] = high
        wprep[t, 0:128, 128:256] = low
        wprep[t, 128:256, 128:256] = low

    er_rows[...] = er_ref[...].T
    pr_rows[...] = pr_ref[...].T
    lane_row = lax.broadcasted_iota(jnp.int32, (1, 128), 1)
    levels = []
    for a in range(2):
        cell = i * 64 + a * 32 + lax.rem(lane_row, 32)
        level = jnp.zeros((1, 128), F32)
        start = jnp.int32(0)
        for k in range(32):
            level = jnp.where(cell >= start, wave_ref[0, k], level)
            start = start + bins_ref[0, k]
        levels.append(level)
    row = lax.broadcasted_iota(jnp.int32, (16, 64), 0)
    pitch = lax.broadcasted_iota(jnp.int32, (16, 64), 1)
    chosen = lax.rem(pitch, 16) == lax.rem(row, 8) * 2 + row // 8
    mask_e = chosen.astype(F32)
    mask_p = (chosen & (pitch < 63)).astype(F32)
    quarter_of = (
        lax.broadcasted_iota(jnp.int32, (64, 128), 0) // 16
        == lax.broadcasted_iota(jnp.int32, (64, 128), 1) // 32
    ).astype(F32)
    sub = lax.broadcasted_iota(jnp.int32, (8, 64), 0)

    def spread(rates, mask):
        wide = (rates[:, None, :] * mask[None]).reshape(128, 64)
        return jnp.dot(
            wide, quarter_of, precision=lax.Precision.HIGHEST, preferred_element_type=F32
        )

    def coefficients(b, _):
        at = pl.ds(pl.multiple_of(b * 8, 8), 8)
        along_e = spread(jnp.where(b * 8 + sub < 127, er_rows[at, :], 0.0), mask_e)
        along_p = spread(pr_rows[at, :], mask_p)
        for a in range(2):
            coef_e[a][at] = (along_e * levels[a]).reshape(8, 2, 8, 128)
            coef_p[a][at] = (along_p * levels[a]).reshape(8, 2, 8, 128)
        return 0

    lax.fori_loop(0, 16, coefficients, 0)
    zero_row = jnp.zeros((2, 8, 128), F32)
    field[0][128] = zero_row
    field[1][128] = zero_row
    other[128] = zero_row

    lanes = lax.broadcasted_iota(jnp.int32, (2, 8, 128), 2)
    far = lanes < 64
    near = lax.rem(lanes, 64) < 32

    def interpolate(rows, t):
        high, low = split(rows)
        both = jnp.dot(
            jnp.concatenate([high, low], axis=1), wprep[t], preferred_element_type=F32
        )
        return both[:, 0:128] + both[:, 128:256]

    def send_on(e, a, place, target):
        pltpu.make_async_remote_copy(
            gath.at[a, e, place],
            field[a].at[i * 4 + e],
            s_c.at[a],
            r_c.at[a],
            device_id=(s, target),
            device_id_type=MESH,
        ).start()

    partner = i + 1 - 2 * lax.rem(i, 2)

    def first_drift(e):
        pltpu.make_async_copy(
            recv1[e].at[pl.ds(0, 21)], recv1[e].at[pl.ds(0, 21)], r_a.at[e]
        ).wait()
        for step in range(16):
            t = lax.rem(i // 2 + 3 * (step + 1), 16)
            moved = interpolate(recv1[e][slot_ref[t]], t).reshape(4, 2, 8, 128)
            outs = turn([moved[q] for q in range(4)], far, near)
            if step < 15:
                for half in range(2):
                    for a in range(2):
                        gath[a, e, step * 2 + half] = outs[half * 2 + a]
                    send_on(e, 0, step * 2 + half, t * 2 + half)
            else:
                odd = lax.rem(i, 2) == 1
                for a in range(2):
                    field[a][i * 4 + e] = jnp.where(odd, outs[2 + a], outs[a])
                    gath[a, e, 30] = jnp.where(odd, outs[a], outs[2 + a])
                send_on(e, 0, 30, partner)

    def send_rest(e):
        def one(step, _):
            t = lax.rem(i // 2 + 3 * (step + 1), 16)
            for half in range(2):
                send_on(e, 1, step * 2 + half, t * 2 + half)
            return 0

        lax.fori_loop(0, 15, one, 0)
        send_on(e, 1, 30, partner)

    first_drift(0)
    send_rest(0)
    first_drift(1)
    first_drift(2)
    send_rest(1)
    first_drift(3)
    send_rest(2)
    send_rest(3)

    sublane = lax.broadcasted_iota(jnp.int32, (8, 128), 0)
    top, bottom = sublane == 0, sublane == 7

    def one_pass(source, target, along_e, along_p):
        def rows(b, carry):
            now, flux_before = carry
            for k in range(32):
                e = b * 32 + k
                later = source[e + 1]
                flux = along_e[e] * (later - now)
                shifted = pltpu.roll(now[0], 7, 0)
                shifted = jnp.where(bottom, pltpu.roll(shifted, 96, 1), shifted)
                pitch_low = along_p[e, 0] * (now[1] - now[0])
                pitch_high = along_p[e, 1] * (shifted - now[1])
                wrapped = pltpu.roll(pitch_high, 1, 0)
                wrapped = jnp.where(top, pltpu.roll(wrapped, 32, 1), wrapped)
                target[e, 0] = now[0] + ((flux[0] - flux_before[0]) + (pitch_low - wrapped))
                target[e, 1] = now[1] + ((flux[1] - flux_before[1]) + (pitch_high - pitch_low))
                now, flux_before = later, flux
            return now, flux_before

        lax.fori_loop(0, 4, rows, (source[0], zero_row))

    def diffuse(a):
        pltpu.make_async_copy(
            field[a].at[pl.ds(0, 124)], field[a].at[pl.ds(0, 124)], r_c.at[a]
        ).wait()

        def two_passes(_, carry):
            one_pass(field[a], other, coef_e[a], coef_p[a])
            one_pass(other, field[a], coef_e[a], coef_p[a])
            return carry

        lax.fori_loop(0, PASSES // 2, two_passes, 0)

    def send_back(a):
        for e in range(4):

            def one(n, _, e=e):
                target = lax.rem(i + 13 * (n + 1), 32)
                pltpu.make_async_remote_copy(
                    field[a].at[target * 4 + e],
                    back[a][e].at[i],
                    s_e.at[a],
                    r_e.at[a, e],
                    device_id=(s, target),
                    device_id_type=MESH,
                ).start()
                return 0

            lax.fori_loop(0, 31, one, 0)
            back[a][e][i] = field[a][i * 4 + e]

    for a in range(2):
        diffuse(a)
        send_back(a)

    def pack_second(a, e):
        here = back[a][e]
        pltpu.make_async_copy(here.at[pl.ds(0, 31)], here.at[pl.ds(0, 31)], r_e.at[a, e]).wait()
        for m in range(8):
            d = sector_at(m)
            for r in range(3):
                tile = pick_ref[d * 3 + r]
                for half in range(2):
                    piece = here[tile * 2 + half]
                    if m < 7:
                        send2[a, e, m, r, half] = piece
                    else:
                        recv2[a][e][s * 3 + r, half] = piece
            if m < 7:
                pltpu.make_async_remote_copy(
                    send2.at[a, e, m],
                    recv2[a][e].at[pl.ds(s * 3, 3)],
                    s_f.at[a],
                    r_f.at[a, e],
                    device_id=(d, i),
                    device_id_type=MESH,
                ).start()

    def second_drift(e):
        for a in range(2):
            there = recv2[a][e]
            pltpu.make_async_copy(
                there.at[pl.ds(0, 21)], there.at[pl.ds(0, 21)], r_f.at[a, e]
            ).wait()
        for t in range(16):
            slot = slot_ref[t]
            pieces = [recv2[a][e][slot] for a in range(2)]
            outs = turn([pieces[a][half] for half in range(2) for a in range(2)], far, near)
            rows = jnp.concatenate([out.reshape(16, 128) for out in outs], axis=0)
            moved = interpolate(rows, t)
            for quarter in range(4):
                for q in range(2):
                    at = quarter * 16 + q * 8
                    order_buf[t, pl.ds(quarter * 16 + q, 8, stride=2), :] = moved[at : at + 8]
            out_ref[e, :, t * 128 : (t + 1) * 128] = order_buf[t]

    for e in range(4):
        pack_second(0, e)
    pack_second(1, 0)
    for e in range(1, 4):
        pack_second(1, e)
        second_drift(e - 1)
    second_drift(3)

    for e in range(4):
        pltpu.make_async_copy(
            send1.at[e, pl.ds(0, 7)], send1.at[e, pl.ds(0, 7)], s_a.at[e]
        ).wait()
    for a in range(2):
        for ref, sem in ((gath, s_c), (send2, s_f)):
            pltpu.make_async_copy(ref.at[a], ref.at[a], sem.at[a]).wait()
        pltpu.make_async_copy(
            field[a].at[pl.ds(0, 124)], field[a].at[pl.ds(0, 124)], s_e.at[a]
        ).wait()


def shards(
    density,
    source_sector,
    source_tile,
    matrix_id,
    cubic_weights,
    bin_cells,
    wave_level,
    energy_rate,
    pitch_rate,
):
    whole = pl.BlockSpec(memory_space=pltpu.VMEM)
    place = pl.BlockSpec(memory_space=pltpu.HBM)
    dma = pltpu.SemaphoreType.DMA

    def vmem(*shape):
        return pltpu.VMEM(shape, F32)

    return pl.pallas_call(
        kernel,
        out_shape=jax.ShapeDtypeStruct((4, 64, 2048), F32),
        in_specs=[place] * 9,
        out_specs=whole,
        scratch_shapes=[
            *[pltpu.SMEM((1, 8, 16), jnp.int32)] * 3,
            pltpu.SMEM((1, 32), jnp.int32),
            pltpu.SMEM((1, 32), F32),
            pltpu.SMEM((24,), jnp.int32),
            pltpu.SMEM((16,), jnp.int32),
            *[vmem(16, 64, 128)] * 4,
            vmem(4, 16, 64, 128),
            vmem(32, 128, 128),
            vmem(64, 128),
            vmem(64, 128),
            vmem(128, 64),
            vmem(128, 64),
            vmem(4, 7, 3, 64, 128),
            *[vmem(24, 64, 128)] * 4,
            vmem(2, 4, 31, 2, 8, 128),
            *[vmem(129, 2, 8, 128)] * 3,
            *[vmem(128, 2, 8, 128)] * 4,
            *[vmem(32, 2, 8, 128)] * 8,
            vmem(2, 4, 7, 3, 2, 2, 8, 128),
            *[vmem(24, 2, 2, 8, 128)] * 8,
            pltpu.VMEM((16, 256, 256), BF16),
            vmem(16, 64, 128),
            dma((5,)),
            dma((4,)),
            dma((3,)),
            dma((4,)),
            dma((4,)),
            dma((2,)),
            dma((2,)),
            dma((2,)),
            dma((2, 4)),
            dma((2,)),
            dma((2, 4)),
        ],
        compiler_params=pltpu.CompilerParams(
            collective_id=0, has_side_effects=True, vmem_limit_bytes=67043328
        ),
        name="ion_step",
    )(
        source_sector,
        source_tile,
        matrix_id,
        bin_cells,
        wave_level,
        density,
        cubic_weights,
        energy_rate.T,
        pitch_rate.T,
    )


def solution(mesh):
    return jax.shard_map(
        shards,
        mesh=mesh,
        in_specs=(
            P("inner", None, "sector"),
            P("inner", None, None),
            P("inner", None, None),
            P("inner", None, None),
            P(),
            P("sector", None),
            P("sector", None),
            P(),
            P(),
        ),
        out_specs=P("inner", None, "sector"),
        check_vma=False,
    )
```

time: 496 us -> 132 us (0.27)
  other arithmetic: 194 us -> 0 us
  Pallas kernels: 0 us -> 129 us
  local copies, waits for them, and re-layouts: 120 us -> 3.14 us
  waiting for transfers between devices: 109 us -> 0 us
  blocking collectives: 42.2 us -> 0 us
  starting transfers between devices: 24.9 us -> 0 us
    pallas_call x0 -> x1, Pallas kernels: none -> 129 us  [shards(): pl.pallas_call(kernel, out_shape=jax.ShapeDtypeStruct((4, 64, 2048), F32)...]
    all_to_all x3 -> x0, waiting for transfers between devices: 109 us -> none  [the longest x1 46.4 us: shards(): lax.all_to_all(packed, 'inner', split_axis=2, concat_axis=0, tiled=True)]
    mul x27 -> x0, other arithmetic: 94.3 us -> none  [the longest x12 65.8 us: one_pass(): flux_p = pitch_rate[:, :-1, None] * (field[:, 1:] - field[:, :-1])]
    gather x9 -> x0, local copies, waits for them, and re-layouts: 48.7 us -> none  [the longest x1 17.5 us: shards(): packed = jnp.take(first, clipped, axis=2) * valid[None, None, :]]
    all_to_all x1 -> x0, blocking collectives: 42.2 us -> none  [drift_step(): lax.all_to_all(outgoing, 'sector', split_axis=2, concat_axis=2, tiled=True)]
    add x13 -> x0, other arithmetic: 36.4 us -> none  [the longest x12 35.7 us: one_pass(): return field + rate_cell[None, None, :] * (change_e + change_p)]
    all_to_all x3 -> x0, starting transfers between devices: 24.9 us -> none  [the longest x1 9.78 us: shards(): lax.all_to_all(packed, 'inner', split_axis=2, concat_axis=0, tiled=True)]
    while x50 -> x0, local copies, waits for them, and re-layouts: 23.2 us -> none
  transfers between devices with their start and end apart: 3 -> 0, of which waited for: 3 -> 0; matrix products, arithmetic and copies ran while one was open for 5% -> 0% of each run, Pallas kernels for 0% -> 0%
where the time goes in v2:
time: 132 us
  Pallas kernels  129 us (98%)
  local copies, waits for them, and re-layouts  3.14 us (2%)
    pallas_call x1, Pallas kernels, shards(): pl.pallas_call(kernel, out_shape=jax.ShapeDtypeStruct((4, 64, 2048), F32)...  129 us
    unnamed x1, local copies, waits for them, and re-layouts  3.14 us

profile of v2, /device:TPU:1, one launch (start us, length us, event | category | flops | bytes accessed | tf_op | source)
XLA Modules:
  0.0 131.7 jit_solution(15729250841911608311)
XLA Ops:
  0.0 128.5 %ion_step.1 = f32[4,64,2048]{2,1,0:T(8,128)} custom-call(s32[1,8,16]{2,1,0:T(8,128)} %refs_0_.1, s32[1,8,16]{2,1,0:T(8,128)} %refs_1_.1, s32[1,8,16]{2,1,0:T(8,128)} %refs_2_.1, s32[1,32]{1,0:T(1,128)} %refs_3_.1, f32[1,32]{1,0:T(1,128)} %refs_4_.1, f32[4,64,2048]{2,1,0:T(8,128)} %refs_5_.1, f32[32,128,128]{2,1,0:T(8,128)} %refs_6_.1, f32[64,128]{1,0:T(8,128)} %bitcast.2, ...), custom_call_target="tpu_custom_call" | custom-call | tf_op jit(solution)/shard_map/ion_step/pallas_call | solution.py:411
  128.6 3.1 %copy.11 = f32[4,64,2048]{2,1,0:T(8,128)} copy(f32[4,64,2048]{2,1,0:T(8,128)} %ion_step.1) | data formatting | bytes 4194304

commit v3 on v2

--- a/solution.py
+++ b/solution.py
@@ -7,6 +7,11 @@
 
 PASSES = 12
 MESH = pl.DeviceIdType.MESH
+FIRST = ((0, 0, 1), (0, 1, 1), (1, 0, 2), (2, 0, 2), (3, 0, 2))
+LAST = (
+    ((0, 0, 2), (1, 0, 2), (2, 0, 2), (3, 0, 2)),
+    ((0, 0, 2), (1, 0, 2), (2, 0, 2), (3, 0, 1), (3, 1, 1)),
+)
 F32 = jnp.float32
 BF16 = jnp.bfloat16
 
@@ -45,16 +50,17 @@
     (out_ref,) = take(1)
     src_ref, tile_ref, mid_ref, bins_ref, wave_ref, pick_ref, slot_ref = take(7)
     natural = take(4)
-    tiles, weight_ref, er_ref, pr_ref, er_rows, pr_rows, send1 = take(7)
-    recv1 = take(4)
-    (gath,) = take(1)
+    tiles, weight_ref, er_ref, pr_ref, er_rows, pr_rows = take(6)
+    send1 = take(5)
+    recv1 = take(5)
+    gath = [take(2) for _ in range(5)]
     field = take(2)
     (other,) = take(1)
     coef_e = take(2)
     coef_p = take(2)
-    back = [take(4) for _ in range(2)]
-    (send2,) = take(1)
-    recv2 = [take(4) for _ in range(2)]
+    back = [take(len(LAST[a])) for a in range(2)]
+    send2 = [take(len(LAST[a])) for a in range(2)]
+    recv2 = [take(len(LAST[a])) for a in range(2)]
     wprep, order_buf = take(2)
     t_sem, d_sem, w_sem, s_a, r_a, s_c, r_c, s_e, r_e, s_f, r_f = take(11)
 
@@ -114,28 +120,33 @@
         for r in range(3):
             pick_ref[d * 3 + r] = picks[r]
 
-    def pack_first(e):
+    def pack_energy(e):
         pltpu.make_async_copy(natural[e], natural[e], d_sem.at[e]).wait()
         for t in range(16):
             for quarter in range(4):
                 for q in range(2):
-                    to = quarter * 16 + q * 8
+                    to = quarter * 8 + q * 32
                     tiles[e, t, to : to + 8, :] = natural[e][
                         t, pl.ds(quarter * 16 + q, 8, stride=2), :
                     ]
-        for m in range(7):
+
+    def pack_first(c):
+        e, q, n = FIRST[c]
+        for m in range(8):
             for r in range(3):
-                send1[e, m, r] = tiles[e, pick_ref[sector_at(m) * 3 + r]]
-        for r in range(3):
-            recv1[e][s * 3 + r] = tiles[e, pick_ref[s * 3 + r]]
-
-    def send_first(e):
+                block = tiles[e, pick_ref[sector_at(m) * 3 + r], 32 * q : 32 * (q + n), :]
+                if m < 7:
+                    send1[c][m, r] = block
+                else:
+                    recv1[c][s * 3 + r] = block
+
+    def send_first(c):
         def one(m, _):
             pltpu.make_async_remote_copy(
-                send1.at[e, m],
-                recv1[e].at[pl.ds(s * 3, 3)],
-                s_a.at[e],
-                r_a.at[e],
+                send1[c].at[m],
+                recv1[c].at[pl.ds(s * 3, 3)],
+                s_a.at[c],
+                r_a.at[c],
                 device_id=(sector_at(m), i),
                 device_id_type=MESH,
             ).start()
@@ -143,12 +154,16 @@
 
         lax.fori_loop(0, 7, one, 0)
 
+    pack_energy(0)
     pack_first(0)
     pl.semaphore_wait(barrier, 38)
     send_first(0)
-    for e in range(1, 4):
-        pack_first(e)
-        send_first(e)
+    pack_first(1)
+    send_first(1)
+    for c in range(2, 5):
+        pack_energy(FIRST[c][0])
+        pack_first(c)
+        send_first(c)
 
     own = [src_ref[0, s, t] for t in range(16)]
     for t in range(16):
@@ -210,9 +225,8 @@
     field[1][128] = zero_row
     other[128] = zero_row
 
-    lanes = lax.broadcasted_iota(jnp.int32, (2, 8, 128), 2)
-    far = lanes < 64
-    near = lax.rem(lanes, 64) < 32
+    lanes = [lax.broadcasted_iota(jnp.int32, (n, 8, 128), 2) for n in (1, 2)]
+    masks = [(lane < 64, lax.rem(lane, 64) < 32) for lane in lanes]
 
     def interpolate(rows, t):
         high, low = split(rows)
@@ -221,11 +235,12 @@
         )
         return both[:, 0:128] + both[:, 128:256]
 
-    def send_on(e, a, place, target):
+    def send_on(c, a, place, target):
+        e, q, n = FIRST[c]
         pltpu.make_async_remote_copy(
-            gath.at[a, e, place],
-            field[a].at[i * 4 + e],
-            s_c.at[a],
+            gath[c][a].at[place],
+            field[a].at[i * 4 + e, pl.ds(q, n)],
+            s_c.at[c, a],
             r_c.at[a],
             device_id=(s, target),
             device_id_type=MESH,
@@ -233,44 +248,49 @@
 
     partner = i + 1 - 2 * lax.rem(i, 2)
 
-    def first_drift(e):
+    def first_drift(c):
+        e, q, n = FIRST[c]
         pltpu.make_async_copy(
-            recv1[e].at[pl.ds(0, 21)], recv1[e].at[pl.ds(0, 21)], r_a.at[e]
+            recv1[c].at[pl.ds(0, 21)], recv1[c].at[pl.ds(0, 21)], r_a.at[c]
         ).wait()
         for step in range(16):
             t = lax.rem(i // 2 + 3 * (step + 1), 16)
-            moved = interpolate(recv1[e][slot_ref[t]], t).reshape(4, 2, 8, 128)
-            outs = turn([moved[q] for q in range(4)], far, near)
+            moved = interpolate(recv1[c][slot_ref[t]], t).reshape(n, 4, 8, 128)
+            outs = turn([moved[:, quarter] for quarter in range(4)], *masks[n - 1])
             if step < 15:
                 for half in range(2):
                     for a in range(2):
-                        gath[a, e, step * 2 + half] = outs[half * 2 + a]
-                    send_on(e, 0, step * 2 + half, t * 2 + half)
+                        gath[c][a][step * 2 + half] = outs[half * 2 + a]
+                    send_on(c, 0, step * 2 + half, t * 2 + half)
             else:
                 odd = lax.rem(i, 2) == 1
                 for a in range(2):
-                    field[a][i * 4 + e] = jnp.where(odd, outs[2 + a], outs[a])
-                    gath[a, e, 30] = jnp.where(odd, outs[a], outs[2 + a])
-                send_on(e, 0, 30, partner)
-
-    def send_rest(e):
+                    field[a][i * 4 + e, q : q + n] = jnp.where(odd, outs[2 + a], outs[a])
+                    gath[c][a][30] = jnp.where(odd, outs[a], outs[2 + a])
+                send_on(c, 0, 30, partner)
+
+    def send_rest(c, begin=0, end=16):
         def one(step, _):
             t = lax.rem(i // 2 + 3 * (step + 1), 16)
             for half in range(2):
-                send_on(e, 1, step * 2 + half, t * 2 + half)
+                send_on(c, 1, step * 2 + half, t * 2 + half)
             return 0
 
-        lax.fori_loop(0, 15, one, 0)
-        send_on(e, 1, 30, partner)
+        lax.fori_loop(begin, min(end, 15), one, 0)
+        if end == 16:
+            send_on(c, 1, 30, partner)
 
     first_drift(0)
     send_rest(0)
     first_drift(1)
+    send_rest(1)
     first_drift(2)
-    send_rest(1)
+    send_rest(2, 0, 8)
     first_drift(3)
-    send_rest(2)
+    send_rest(2, 8, 16)
+    first_drift(4)
     send_rest(3)
+    send_rest(4)
 
     sublane = lax.broadcasted_iota(jnp.int32, (8, 128), 0)
     top, bottom = sublane == 0, sublane == 7
@@ -308,30 +328,31 @@
         lax.fori_loop(0, PASSES // 2, two_passes, 0)
 
     def send_back(a):
-        for e in range(4):
-
-            def one(n, _, e=e):
-                target = lax.rem(i + 13 * (n + 1), 32)
+        for c, (e, q, n) in enumerate(LAST[a]):
+            rows = pl.ds(q, n)
+
+            def one(k, _, c=c, e=e, rows=rows):
+                target = lax.rem(i + 13 * (k + 1), 32)
                 pltpu.make_async_remote_copy(
-                    field[a].at[target * 4 + e],
-                    back[a][e].at[i],
+                    field[a].at[target * 4 + e, rows],
+                    back[a][c].at[i],
                     s_e.at[a],
-                    r_e.at[a, e],
+                    r_e.at[a, c],
                     device_id=(s, target),
                     device_id_type=MESH,
                 ).start()
                 return 0
 
             lax.fori_loop(0, 31, one, 0)
-            back[a][e][i] = field[a][i * 4 + e]
+            back[a][c][i] = field[a][i * 4 + e, q : q + n]
 
     for a in range(2):
         diffuse(a)
         send_back(a)
 
-    def pack_second(a, e):
-        here = back[a][e]
-        pltpu.make_async_copy(here.at[pl.ds(0, 31)], here.at[pl.ds(0, 31)], r_e.at[a, e]).wait()
+    def pack_second(a, c):
+        here = back[a][c]
+        pltpu.make_async_copy(here.at[pl.ds(0, 31)], here.at[pl.ds(0, 31)], r_e.at[a, c]).wait()
         for m in range(8):
             d = sector_at(m)
             for r in range(3):
@@ -339,52 +360,62 @@
                 for half in range(2):
                     piece = here[tile * 2 + half]
                     if m < 7:
-                        send2[a, e, m, r, half] = piece
+                        send2[a][c][m, r, half] = piece
                     else:
-                        recv2[a][e][s * 3 + r, half] = piece
+                        recv2[a][c][s * 3 + r, half] = piece
             if m < 7:
                 pltpu.make_async_remote_copy(
-                    send2.at[a, e, m],
-                    recv2[a][e].at[pl.ds(s * 3, 3)],
-                    s_f.at[a],
-                    r_f.at[a, e],
+                    send2[a][c].at[m],
+                    recv2[a][c].at[pl.ds(s * 3, 3)],
+                    s_f.at[a, c],
+                    r_f.at[a, c],
                     device_id=(d, i),
                     device_id_type=MESH,
                 ).start()
 
-    def second_drift(e):
-        for a in range(2):
-            there = recv2[a][e]
-            pltpu.make_async_copy(
-                there.at[pl.ds(0, 21)], there.at[pl.ds(0, 21)], r_f.at[a, e]
-            ).wait()
+    def arrive(a, c):
+        there = recv2[a][c]
+        pltpu.make_async_copy(
+            there.at[pl.ds(0, 21)], there.at[pl.ds(0, 21)], r_f.at[a, c]
+        ).wait()
+
+    def second_drift(c):
+        e, q, n = LAST[1][c]
+        if q == 0:
+            arrive(0, e)
+        arrive(1, c)
         for t in range(16):
             slot = slot_ref[t]
-            pieces = [recv2[a][e][slot] for a in range(2)]
-            outs = turn([pieces[a][half] for half in range(2) for a in range(2)], far, near)
-            rows = jnp.concatenate([out.reshape(16, 128) for out in outs], axis=0)
+            first, second = recv2[0][e][slot], recv2[1][c][slot]
+            outs = turn(
+                [first[0, q : q + n], second[0], first[1, q : q + n], second[1]], *masks[n - 1]
+            )
+            rows = jnp.stack(outs, axis=1).reshape(32 * n, 128)
             moved = interpolate(rows, t)
             for quarter in range(4):
-                for q in range(2):
-                    at = quarter * 16 + q * 8
-                    order_buf[t, pl.ds(quarter * 16 + q, 8, stride=2), :] = moved[at : at + 8]
-            out_ref[e, :, t * 128 : (t + 1) * 128] = order_buf[t]
-
-    for e in range(4):
-        pack_second(0, e)
+                for k in range(n):
+                    at = quarter * 8 + k * 32
+                    order_buf[e, t, pl.ds(quarter * 16 + q + k, 8, stride=2), :] = moved[
+                        at : at + 8
+                    ]
+            if q + n == 2:
+                out_ref[e, :, t * 128 : (t + 1) * 128] = order_buf[e, t]
+
+    for c in range(4):
+        pack_second(0, c)
     pack_second(1, 0)
-    for e in range(1, 4):
-        pack_second(1, e)
-        second_drift(e - 1)
-    second_drift(3)
-
-    for e in range(4):
-        pltpu.make_async_copy(
-            send1.at[e, pl.ds(0, 7)], send1.at[e, pl.ds(0, 7)], s_a.at[e]
-        ).wait()
+    for c in range(1, 5):
+        pack_second(1, c)
+        second_drift(c - 1)
+    second_drift(4)
+
+    for c in range(5):
+        pltpu.make_async_copy(send1[c], send1[c], s_a.at[c]).wait()
+        for a in range(2):
+            pltpu.make_async_copy(gath[c][a], gath[c][a], s_c.at[c, a]).wait()
     for a in range(2):
-        for ref, sem in ((gath, s_c), (send2, s_f)):
-            pltpu.make_async_copy(ref.at[a], ref.at[a], sem.at[a]).wait()
+        for c in range(len(LAST[a])):
+            pltpu.make_async_copy(send2[a][c], send2[a][c], s_f.at[a, c]).wait()
         pltpu.make_async_copy(
             field[a].at[pl.ds(0, 124)], field[a].at[pl.ds(0, 124)], s_e.at[a]
         ).wait()
@@ -401,7 +432,6 @@
     energy_rate,
     pitch_rate,
 ):
-    whole = pl.BlockSpec(memory_space=pltpu.VMEM)
     place = pl.BlockSpec(memory_space=pltpu.HBM)
     dma = pltpu.SemaphoreType.DMA
 
@@ -412,7 +442,7 @@
         kernel,
         out_shape=jax.ShapeDtypeStruct((4, 64, 2048), F32),
         in_specs=[place] * 9,
-        out_specs=whole,
+        out_specs=pl.BlockSpec(memory_space=pltpu.VMEM),
         scratch_shapes=[
             *[pltpu.SMEM((1, 8, 16), jnp.int32)] * 3,
             pltpu.SMEM((1, 32), jnp.int32),
@@ -426,42 +456,47 @@
             vmem(64, 128),
             vmem(128, 64),
             vmem(128, 64),
-            vmem(4, 7, 3, 64, 128),
-            *[vmem(24, 64, 128)] * 4,
-            vmem(2, 4, 31, 2, 8, 128),
+            *[vmem(7, 3, 32 * n, 128) for _, _, n in FIRST],
+            *[vmem(24, 32 * n, 128) for _, _, n in FIRST],
+            *[vmem(31, n, 8, 128) for _, _, n in FIRST for _ in range(2)],
             *[vmem(129, 2, 8, 128)] * 3,
             *[vmem(128, 2, 8, 128)] * 4,
-            *[vmem(32, 2, 8, 128)] * 8,
-            vmem(2, 4, 7, 3, 2, 2, 8, 128),
-            *[vmem(24, 2, 2, 8, 128)] * 8,
+            *[vmem(32, n, 8, 128) for pieces in LAST for _, _, n in pieces],
+            *[vmem(7, 3, 2, n, 8, 128) for pieces in LAST for _, _, n in pieces],
+            *[vmem(24, 2, n, 8, 128) for pieces in LAST for _, _, n in pieces],
             pltpu.VMEM((16, 256, 256), BF16),
-            vmem(16, 64, 128),
+            vmem(4, 16, 64, 128),
             dma((5,)),
             dma((4,)),
             dma((3,)),
-            dma((4,)),
-            dma((4,)),
+            dma((5,)),
+            dma((5,)),
+            dma((5, 2)),
             dma((2,)),
             dma((2,)),
-            dma((2,)),
-            dma((2, 4)),
-            dma((2,)),
-            dma((2, 4)),
+            dma((2, 5)),
+            dma((2, 5)),
+            dma((2, 5)),
         ],
         compiler_params=pltpu.CompilerParams(
-            collective_id=0, has_side_effects=True, vmem_limit_bytes=67043328
+            collective_id=0, has_side_effects=True, vmem_limit_bytes=50 * 2**20
         ),
         name="ion_step",
     )(
-        source_sector,
-        source_tile,
-        matrix_id,
-        bin_cells,
-        wave_level,
-        density,
-        cubic_weights,
-        energy_rate.T,
-        pitch_rate.T,
+        *[
+            pltpu.with_memory_space_constraint(operand, pltpu.HBM)
+            for operand in (
+                source_sector,
+                source_tile,
+                matrix_id,
+                bin_cells,
+                wave_level,
+                density,
+                cubic_weights,
+                energy_rate.T,
+                pitch_rate.T,
+            )
+        ]
     )
 
 

time: 132 us -> 127 us (0.962)
  Pallas kernels: 129 us -> 125 us
  local copies, waits for them, and re-layouts: 3.14 us -> 1.32 us
    pallas_call x1, Pallas kernels: 129 us -> 125 us  [shards(): pl.pallas_call(kernel, out_shape=jax.ShapeDtypeStruct((4, 64, 2048), F32)...]
    unnamed x1, local copies, waits for them, and re-layouts: 3.14 us -> 1.32 us
where the time goes in v3:
time: 127 us
  Pallas kernels  125 us (98%)
  local copies, waits for them, and re-layouts  1.32 us (1%)
    pallas_call x1, Pallas kernels, shards(): pl.pallas_call(kernel, out_shape=jax.ShapeDtypeStruct((4, 64, 2048), F32)...  125 us

profile of v3, /device:TPU:1, one launch (start us, length us, event | category | flops | bytes accessed | tf_op | source)
XLA Modules:
  0.0 126.8 jit_solution(16894556861461711350)
XLA Ops:
  0.0 125.5 %ion_step.1 = f32[4,64,2048]{2,1,0:T(8,128)S(1)} custom-call(s32[1,8,16]{2,1,0:T(8,128)} %refs_0_.1, s32[1,8,16]{2,1,0:T(8,128)} %refs_1_.1, s32[1,8,16]{2,1,0:T(8,128)} %refs_2_.1, s32[1,32]{1,0:T(1,128)} %refs_3_.1, f32[1,32]{1,0:T(1,128)} %refs_4_.1, f32[4,64,2048]{2,1,0:T(8,128)} %refs_5_.1, f32[32,128,128]{2,1,0:T(8,128)} %refs_6_.1, ...), custom_call_target="tpu_custom_call" | custom-call | tf_op jit(solution)/shard_map/ion_step/pallas_call | solution.py:441
  125.5 1.3 %copy.11 = f32[4,64,2048]{2,1,0:T(8,128)} copy(f32[4,64,2048]{2,1,0:T(8,128)S(1)} %ion_step.1) | data formatting | bytes 4194304

commit v4 on v3

--- a/solution.py
+++ b/solution.py
@@ -6,6 +6,7 @@
 from jax.sharding import PartitionSpec as P
 
 PASSES = 12
+STRIDE = 8
 MESH = pl.DeviceIdType.MESH
 FIRST = ((0, 0, 1), (0, 1, 1), (1, 0, 2), (2, 0, 2), (3, 0, 2))
 LAST = (
@@ -58,6 +59,8 @@
     (other,) = take(1)
     coef_e = take(2)
     coef_p = take(2)
+    coef_d = take(2)
+    above, beneath = take(2)
     back = [take(len(LAST[a])) for a in range(2)]
     send2 = [take(len(LAST[a])) for a in range(2)]
     recv2 = [take(len(LAST[a])) for a in range(2)]
@@ -210,13 +213,27 @@
             wide, quarter_of, precision=lax.Precision.HIGHEST, preferred_element_type=F32
         )
 
+    sublane = lax.broadcasted_iota(jnp.int32, (8, 128), 0)
+    top, bottom = sublane == 0, sublane == 7
+
+    def from_above(block):
+        block = pltpu.roll(block, 7, 0)
+        return jnp.where(bottom, pltpu.roll(block, 96, 1), block)
+
+    def from_below(block):
+        block = pltpu.roll(block, 1, 0)
+        return jnp.where(top, pltpu.roll(block, 32, 1), block)
+
     def coefficients(b, _):
         at = pl.ds(pl.multiple_of(b * 8, 8), 8)
         along_e = spread(jnp.where(b * 8 + sub < 127, er_rows[at, :], 0.0), mask_e)
         along_p = spread(pr_rows[at, :], mask_p)
         for a in range(2):
             coef_e[a][at] = (along_e * levels[a]).reshape(8, 2, 8, 128)
-            coef_p[a][at] = (along_p * levels[a]).reshape(8, 2, 8, 128)
+            scaled = (along_p * levels[a]).reshape(8, 2, 8, 128)
+            coef_p[a][at] = scaled
+            for k in range(8):
+                coef_d[a][b * 8 + k] = from_below(scaled[k, 1])
         return 0
 
     lax.fori_loop(0, 16, coefficients, 0)
@@ -287,42 +304,49 @@
     first_drift(2)
     send_rest(2, 0, 8)
     first_drift(3)
+    first_drift(4)
     send_rest(2, 8, 16)
-    first_drift(4)
     send_rest(3)
     send_rest(4)
 
-    sublane = lax.broadcasted_iota(jnp.int32, (8, 128), 0)
-    top, bottom = sublane == 0, sublane == 7
-
-    def one_pass(source, target, along_e, along_p):
-        def rows(b, carry):
-            now, flux_before = carry
-            for k in range(32):
-                e = b * 32 + k
-                later = source[e + 1]
-                flux = along_e[e] * (later - now)
-                shifted = pltpu.roll(now[0], 7, 0)
-                shifted = jnp.where(bottom, pltpu.roll(shifted, 96, 1), shifted)
-                pitch_low = along_p[e, 0] * (now[1] - now[0])
-                pitch_high = along_p[e, 1] * (shifted - now[1])
-                wrapped = pltpu.roll(pitch_high, 1, 0)
-                wrapped = jnp.where(top, pltpu.roll(wrapped, 32, 1), wrapped)
-                target[e, 0] = now[0] + ((flux[0] - flux_before[0]) + (pitch_low - wrapped))
-                target[e, 1] = now[1] + ((flux[1] - flux_before[1]) + (pitch_high - pitch_low))
-                now, flux_before = later, flux
-            return now, flux_before
-
-        lax.fori_loop(0, 4, rows, (source[0], zero_row))
+    def neighbours(ref, base, shift):
+        for k in range(shift, shift + STRIDE):
+            above[base + k] = from_above(ref[base + k, 0])
+            beneath[base + k] = from_below(ref[base + k, 1])
+
+    def advance(source, target, a, base, carry):
+        now, flux_before = carry
+        for k in range(STRIDE):
+            e = base + k
+            later = source[e + 1]
+            flux = coef_e[a][e] * (later - now)
+            low = coef_p[a][e, 0] * (now[1] - now[0])
+            high = coef_p[a][e, 1] * (above[e] - now[1])
+            under = coef_d[a][e] * (now[0] - beneath[e])
+            target[e, 0] = now[0] + ((flux[0] - flux_before[0]) + (low - under))
+            target[e, 1] = now[1] + ((flux[1] - flux_before[1]) + (high - low))
+            now, flux_before = later, flux
+        return now, flux_before
+
+    def one_pass(source, target, a):
+        carry = (source[0], zero_row)
+        for base in range(0, 128, STRIDE):
+            if base + STRIDE < 128:
+                neighbours(source, base, STRIDE)
+            else:
+                neighbours(target, 0, 0)
+            carry = advance(source, target, a, base, carry)
 
     def diffuse(a):
         pltpu.make_async_copy(
             field[a].at[pl.ds(0, 124)], field[a].at[pl.ds(0, 124)], r_c.at[a]
         ).wait()
 
+        neighbours(field[a], 0, 0)
+
         def two_passes(_, carry):
-            one_pass(field[a], other, coef_e[a], coef_p[a])
-            one_pass(other, field[a], coef_e[a], coef_p[a])
+            one_pass(field[a], other, a)
+            one_pass(other, field[a], a)
             return carry
 
         lax.fori_loop(0, PASSES // 2, two_passes, 0)
@@ -461,6 +485,7 @@
             *[vmem(31, n, 8, 128) for _, _, n in FIRST for _ in range(2)],
             *[vmem(129, 2, 8, 128)] * 3,
             *[vmem(128, 2, 8, 128)] * 4,
+            *[vmem(128, 8, 128)] * 4,
             *[vmem(32, n, 8, 128) for pieces in LAST for _, _, n in pieces],
             *[vmem(7, 3, 2, n, 8, 128) for pieces in LAST for _, _, n in pieces],
             *[vmem(24, 2, n, 8, 128) for pieces in LAST for _, _, n in pieces],

time: 127 us -> 125 us (0.984)
  Pallas kernels: 125 us -> 123 us
    pallas_call x1, Pallas kernels: 125 us -> 123 us  [shards(): pl.pallas_call(kernel, out_shape=jax.ShapeDtypeStruct((4, 64, 2048), F32)...]
where the time goes in v4:
time: 125 us
  Pallas kernels  123 us (98%)
  local copies, waits for them, and re-layouts  1.32 us (1%)
    pallas_call x1, Pallas kernels, shards(): pl.pallas_call(kernel, out_shape=jax.ShapeDtypeStruct((4, 64, 2048), F32)...  123 us

profile of v4, /device:TPU:1, one launch (start us, length us, event | category | flops | bytes accessed | tf_op | source)
XLA Modules:
  0.0 124.6 jit_solution(15761231487242085923)
XLA Ops:
  0.0 123.3 %ion_step.1 = f32[4,64,2048]{2,1,0:T(8,128)S(1)} custom-call(s32[1,8,16]{2,1,0:T(8,128)} %refs_0_.1, s32[1,8,16]{2,1,0:T(8,128)} %refs_1_.1, s32[1,8,16]{2,1,0:T(8,128)} %refs_2_.1, s32[1,32]{1,0:T(1,128)} %refs_3_.1, f32[1,32]{1,0:T(1,128)} %refs_4_.1, f32[4,64,2048]{2,1,0:T(8,128)} %refs_5_.1, f32[32,128,128]{2,1,0:T(8,128)} %refs_6_.1, ...), custom_call_target="tpu_custom_call" | custom-call | tf_op jit(solution)/shard_map/ion_step/pallas_call | solution.py:465
  123.3 1.3 %copy.11 = f32[4,64,2048]{2,1,0:T(8,128)} copy(f32[4,64,2048]{2,1,0:T(8,128)S(1)} %ion_step.1) | data formatting | bytes 4194304

commit v5 on v4

--- a/solution.py
+++ b/solution.py
@@ -95,19 +95,13 @@
     ]
     for copy in tables:
         copy.start()
-    for e in range(4):
+    def fetch(e):
         for t in range(16):
             pltpu.make_async_copy(
                 dens_in.at[e, :, t * 128 : (t + 1) * 128], natural[e].at[t], d_sem.at[e]
             ).start()
-    parameters = [
-        pltpu.make_async_copy(a, b, w_sem.at[n])
-        for n, (a, b) in enumerate(
-            ((weight_in, weight_ref), (er_in, er_ref), (pr_in, pr_ref))
-        )
-    ]
-    for copy in parameters:
-        copy.start()
+
+    fetch(0)
     for copy in tables:
         copy.wait()
 
@@ -163,6 +157,16 @@
     send_first(0)
     pack_first(1)
     send_first(1)
+    for e in range(1, 4):
+        fetch(e)
+    parameters = [
+        pltpu.make_async_copy(a, b, w_sem.at[n])
+        for n, (a, b) in enumerate(
+            ((weight_in, weight_ref), (er_in, er_ref), (pr_in, pr_ref))
+        )
+    ]
+    for copy in parameters:
+        copy.start()
     for c in range(2, 5):
         pack_energy(FIRST[c][0])
         pack_first(c)

time: 125 us -> 125 us (level)
  no operation moved by 1% of the time
where the time goes in v5:
time: 125 us
  Pallas kernels  123 us (98%)
  local copies, waits for them, and re-layouts  1.32 us (1%)
    pallas_call x1, Pallas kernels, shards(): pl.pallas_call(kernel, out_shape=jax.ShapeDtypeStruct((4, 64, 2048), F32)...  123 us

profile of v5, /device:TPU:1, one launch (start us, length us, event | category | flops | bytes accessed | tf_op | source)
XLA Modules:
  0.0 124.6 jit_solution(3212997694828340053)
XLA Ops:
  0.0 123.2 %ion_step.1 = f32[4,64,2048]{2,1,0:T(8,128)S(1)} custom-call(s32[1,8,16]{2,1,0:T(8,128)} %refs_0_.1, s32[1,8,16]{2,1,0:T(8,128)} %refs_1_.1, s32[1,8,16]{2,1,0:T(8,128)} %refs_2_.1, s32[1,32]{1,0:T(1,128)} %refs_3_.1, f32[1,32]{1,0:T(1,128)} %refs_4_.1, f32[4,64,2048]{2,1,0:T(8,128)} %refs_5_.1, f32[32,128,128]{2,1,0:T(8,128)} %refs_6_.1, ...), custom_call_target="tpu_custom_call" | custom-call | tf_op jit(solution)/shard_map/ion_step/pallas_call | solution.py:469
  123.3 1.3 %copy.11 = f32[4,64,2048]{2,1,0:T(8,128)} copy(f32[4,64,2048]{2,1,0:T(8,128)S(1)} %ion_step.1) | data formatting | bytes 4194304
